TPU v7x, 128 devices: a whole 4x4x4 slice. The times are simulated.
128 devices in a mesh: rep: 4 (over x), shard: 32 (over z, y, core).
Axes of the slice: x: 4, y: 4, z: 4, core: 2. Of those that a mesh axis runs over, the one named last changes fastest.
Arguments:
- attention_grad: bfloat16 [4, 8, 768, 768], P('rep', None, 'shard'), may hold values from -45 to 45
- dense_grad: bfloat16 [4, 2, 3072, 768], P('rep', None, 'shard'), may hold values from -45 to 45
- embedding_grad: bfloat16 [4, 8192, 768], P('rep', 'shard'), may hold values from -45 to 45
- attention_error: float32 [4, 8, 768, 768], P('rep', None, 'shard'), may hold values from -4 to 4
- dense_error: float32 [4, 2, 3072, 768], P('rep', None, 'shard'), may hold values from -4 to 4
- embedding_error: float32 [4, 8192, 768], P('rep', 'shard'), may hold values from -4 to 4
- attention_weight: float32 [8, 768, 768], P(None, 'shard'), may hold values from -0.21875 to 0.21875
- dense_weight: float32 [2, 3072, 768], P(None, 'shard'), may hold values from -0.21875 to 0.21875
- embedding_weight: float32 [8192, 768], P('shard'), may hold values from -0.21875 to 0.21875
- attention_momentum: float32 [8, 768, 768], P(None, 'shard'), may hold values from -1.5 to 1.5
- dense_momentum: float32 [2, 3072, 768], P(None, 'shard'), may hold values from -1.5 to 1.5
- embedding_momentum: float32 [8192, 768], P('shard'), may hold values from -1.5 to 1.5
- warm_start: float32 [11, 32, 768], replicated, may hold values from -0.21875 to 0.21875
- norm_scale: float32 [3, 768], P(None, 'shard'), may hold values from 0.5 to 1.5
- norm_momentum: float32 [3, 768], P(None, 'shard'), may hold values from -1.5 to 1.5
- norm_grad: float32 [4, 3, 768], P('rep', None, 'shard'), may hold values from -6 to 6
Outputs:
- attention_updated: float32 [8, 768, 768], P(None, 'shard')
- dense_updated: float32 [2, 3072, 768], P(None, 'shard')
- embedding_updated: float32 [8192, 768], P('shard')
- attention_copy: bfloat16 [8, 768, 768], P(None, 'shard')
- dense_copy: bfloat16 [2, 3072, 768], P(None, 'shard')
- embedding_copy: bfloat16 [8192, 768], P('shard')
- attention_residue: float32 [4, 8, 768, 768], P('rep', None, 'shard')
- dense_residue: float32 [4, 2, 3072, 768], P('rep', None, 'shard')
- embedding_residue: float32 [4, 8192, 768], P('rep', 'shard')
- attention_velocity: float32 [8, 768, 768], P(None, 'shard')
- dense_velocity: float32 [2, 3072, 768], P(None, 'shard')
- embedding_velocity: float32 [8192, 768], P('shard')
- next_start: float32 [11, 32, 768], replicated
- norm_updated: float32 [3, 768], P(None, 'shard')
- norm_velocity: float32 [3, 768], P(None, 'shard')
All inputs are finite; a program needn't handle non-finite values.
Results may differ from a plain program's by a relative error of at most 0.001.
Values sent between devices are 32-bit elements; how exact they have to be, the bound alone decides.
A program may use at most 64 MiB of HBM per device.

v0:
```python
import jax
import jax.numpy as jnp
from jax import lax
from jax.sharding import PartitionSpec as P


def invert(grams):
    factor = jnp.linalg.cholesky(grams)
    identity = jnp.broadcast_to(jnp.eye(grams.shape[-1], dtype=grams.dtype), grams.shape)
    return lax.linalg.triangular_solve(factor, identity, left_side=True, lower=True)


def finish(merged, approx, weight, momentum):
    velocity = 0.9 * momentum + approx
    updated = weight - 0.05 * velocity
    return (updated, updated.astype(jnp.bfloat16), (merged - approx)[None], velocity)


def body(
    attention_grad,
    dense_grad,
    embedding_grad,
    attention_error,
    dense_error,
    embedding_error,
    attention_weight,
    dense_weight,
    embedding_weight,
    attention_momentum,
    dense_momentum,
    embedding_momentum,
    warm_start,
    norm_scale,
    norm_momentum,
    norm_grad,
):
    highest = lax.Precision.HIGHEST
    replicas = lax.axis_size("rep")
    norm_total = lax.psum(norm_grad[0], "rep")
    merged_attention = attention_grad[0].astype(jnp.float32) + attention_error[0]
    merged_dense = dense_grad[0].astype(jnp.float32) + dense_error[0]
    merged_embedding = embedding_grad[0].astype(jnp.float32) + embedding_error[0]
    proj_attention = jnp.einsum("mkc,mrc->mkr", warm_start[:8], merged_attention, precision=highest)
    proj_dense = jnp.einsum("mkc,mrc->mkr", warm_start[8:10], merged_dense, precision=highest)
    proj_embedding = jnp.einsum("kc,rc->kr", warm_start[10], merged_embedding, precision=highest)
    proj_attention, proj_dense, proj_embedding = lax.psum(
        (proj_attention, proj_dense, proj_embedding), "rep"
    )
    proj_attention = proj_attention / replicas
    proj_dense = proj_dense / replicas
    proj_embedding = proj_embedding / replicas
    local_grams = jnp.concatenate(
        [
            jnp.einsum("mkr,mjr->mkj", proj_attention, proj_attention, precision=highest),
            jnp.einsum("mkr,mjr->mkj", proj_dense, proj_dense, precision=highest),
            jnp.einsum("kr,jr->kj", proj_embedding, proj_embedding, precision=highest)[None],
        ],
        0,
    )
    grams = lax.psum(local_grams, "shard")
    inverse = invert(grams)
    ortho_attention = jnp.einsum("mjk,mkr->mjr", inverse[:8], proj_attention, precision=highest)
    ortho_dense = jnp.einsum("mjk,mkr->mjr", inverse[8:10], proj_dense, precision=highest)
    ortho_embedding = jnp.einsum("jk,kr->jr", inverse[10], proj_embedding, precision=highest)
    partial_right = jnp.concatenate(
        [
            jnp.einsum("mkr,mrc->mkc", ortho_attention, merged_attention, precision=highest),
            jnp.einsum("mkr,mrc->mkc", ortho_dense, merged_dense, precision=highest),
            jnp.einsum("kr,rc->kc", ortho_embedding, merged_embedding, precision=highest)[None],
        ],
        0,
    )
    next_start = lax.psum(partial_right, ("rep", "shard")) / replicas
    approx_attention = jnp.einsum(
        "mkr,mkc->mrc", ortho_attention, next_start[:8], precision=highest
    )
    approx_dense = jnp.einsum("mkr,mkc->mrc", ortho_dense, next_start[8:10], precision=highest)
    approx_embedding = jnp.einsum("kr,kc->rc", ortho_embedding, next_start[10], precision=highest)
    a_upd, a_copy, a_res, a_vel = finish(
        merged_attention, approx_attention, attention_weight, attention_momentum
    )
    d_upd, d_copy, d_res, d_vel = finish(merged_dense, approx_dense, dense_weight, dense_momentum)
    e_upd, e_copy, e_res, e_vel = finish(
        merged_embedding, approx_embedding, embedding_weight, embedding_momentum
    )
    norm_velocity = 0.9 * norm_momentum + norm_total / replicas
    norm_updated = norm_scale - 0.05 * norm_velocity
    return (
        a_upd,
        d_upd,
        e_upd,
        a_copy,
        d_copy,
        e_copy,
        a_res,
        d_res,
        e_res,
        a_vel,
        d_vel,
        e_vel,
        next_start,
        norm_updated,
        norm_velocity,
    )


def solution(mesh):
    return jax.shard_map(
        body,
        mesh=mesh,
        in_specs=(
            P("rep", None, "shard", None),
            P("rep", None, "shard", None),
            P("rep", "shard", None),
            P("rep", None, "shard", None),
            P("rep", None, "shard", None),
            P("rep", "shard", None),
            P(None, "shard", None),
            P(None, "shard", None),
            P("shard", None),
            P(None, "shard", None),
            P(None, "shard", None),
            P("shard", None),
            P(),
            P(None, "shard"),
            P(None, "shard"),
            P("rep", None, "shard"),
        ),
        out_specs=(
            P(None, "shard", None),
            P(None, "shard", None),
            P("shard", None),
            P(None, "shard", None),
            P(None, "shard", None),
            P("shard", None),
            P("rep", None, "shard", None),
            P("rep", None, "shard", None),
            P("rep", "shard", None),
            P(None, "shard", None),
            P(None, "shard", None),
            P("shard", None),
            P(),
            P(None, "shard"),
            P(None, "shard"),
        ),
        check_vma=False,
    )
```

profile of v0, /device:TPU:1, one launch (start us, length us, event | category | flops | bytes accessed | tf_op | source)
XLA Modules:
  0.0 417.3 jit_solution(11912199704461353907)
XLA Ops:
  7.2 1.3 copy.47
  8.6 2.7 convolution_bitcast_fusion.2
  11.3 2.2 convolution_bitcast_fusion.3
  13.5 2.6 convolution_bitcast_fusion
  16.2 41.9 %all-reduce.6.cloned.1.call-done = (f32[32,256]{1,0:T(8,128)}, f32[2,32,96]{2,1,0:T(8,128)}, f32[8,32,24]{1,2,0:T(8,128)}, f32[3,24]{1,0:T(4,128)}) async-done(((f32[32,256]{1,0:T(8,128)}, f32[2,32,96]{2,1,0:T(8,128)}, f32[8,32,24]{1,2,0:T(8,128)}, f32[3,24]{1,0:T(4,128)}), (f32[32,256]{1,0:T(8,128)}, f32[2,32,96]{2,1,0:T(8,128)}, f32[8,32,24]{1,2,0:T(8,128)}, ...) | async-done | bytes 82224 | tf_op jit(solution)/shard_map/psum | solution.py:46
  58.2 1.0 convolution_bitcast_fusion.4
  59.2 1.0 fusion.35
  60.2 1.4 fusion.25
  61.6 125.0 %psum.45 = f32[11,32,32]{1,2,0:T(8,128)S(1)} all-reduce(f32[11,32,32]{1,2,0:T(8,128)S(1)} %pad_maximum_fusion.1), channel_id=1, replica_groups=mesh['rep'=4,'shard'=32] {'shard'}, use_global_device_ids=true, to_apply=%region_3.0 | all-reduce | flops 11264 | bytes 90112 | tf_op jit(solution)/shard_map/psum | solution.py:60
  186.7 0.7 fusion.19
  187.4 32.9 %custom-call.7 = f32[11,32,32]{2,1,0:T(8,128)S(1)} custom-call(f32[11,32,32]{2,1,0:T(8,128)} %fusion.19), custom_call_target="Cholesky" | custom-call | tf_op jit(solution)/shard_map/jit(cholesky)/cholesky | solution.py:8
  220.6 27.1 %custom-call.8 = f32[11,1,32,32]{2,3,1,0:T(8,128)S(1)} custom-call(f32[11,1,32,32]{3,2,1,0:T(8,128)S(1)} %select_bitcast_fusion), custom_call_target="InvertDiagBlocksLowerTriangular" | custom-call | tf_op jit(solution)/shard_map/triangular_solve | solution.py:10
  248.5 0.9 fusion.30
  249.5 0.9 fusion.33
  250.4 0.6 convolution_bitcast_fusion.1
  251.5 0.8 fusion.10
  252.3 1.1 pad_maximum_fusion
  253.4 0.7 copy-done.14
  254.1 0.6 multiply_subtract_fusion.3
  254.7 147.5 %all-reduce.4.cloned.1.call-done = f32[11,32,768]{2,1,0:T(8,128)} async-done(((f32[11,32,768]{2,1,0:T(8,128)}), f32[11,32,768]{2,1,0:T(8,128)}) %all-reduce.4.cloned.1.call-update) | async-done | bytes 1081360 | tf_op jit(solution)/shard_map/psum | solution.py:73
  402.2 1.4 broadcast_multiply_fusion
  403.7 2.1 fusion.50
  405.8 2.1 fusion.49
  407.9 2.5 fusion.48
  (48 shorter events, 2.0 us)
Async XLA Ops:
  7.2 4.1 copy-start.2
  7.2 4.1 copy-start.6
  7.2 51.0 %all-reduce.6.cloned.1.call-start = ((), (), s32[]{:S(2)}) async-start(), calls=%async_computation.1 | async-start | bytes 331776 | tf_op jit(solution)/shard_map/psum | solution.py:46
  8.6 4.9 %copy-start.1 = (f32[1,8,24,768]{3,2,1,0:T(8,128)S(1)}, f32[1,8,24,768]{3,2,1,0:T(8,128)}, u32[]{:S(2)}) copy-start(f32[1,8,24,768]{3,2,1,0:T(8,128)} %param.19) | copy-start | bytes 1769476
  8.6 4.9 %copy-start.5 = (bf16[1,8,24,768]{3,2,1,0:T(8,128)(2,1)S(1)}, bf16[1,8,24,768]{3,2,1,0:T(8,128)(2,1)}, u32[]{:S(2)}) copy-start(bf16[1,8,24,768]{3,2,1,0:T(8,128)(2,1)} %param.16) | copy-start | bytes 884740
  16.1 386.0 %all-reduce.4.cloned.1.call-start = ((), (), s32[]{:S(2)}) async-start(), calls=%async_computation | async-start | bytes 2162688 | tf_op jit(solution)/shard_map/psum | solution.py:73
  61.6 186.6 %copy-start.13 = (f32[8,32,24]{1,2,0:T(8,128)S(1)}, f32[8,32,24]{1,2,0:T(8,128)}, u32[]{:S(2)}) copy-start(f32[8,32,24]{1,2,0:T(8,128)} %get-tuple-element.17) | copy-start | bytes 73732
  186.7 63.7 %copy-start = (f32[1,256,768]{2,1,0:T(8,128)S(1)}, f32[1,256,768]{2,1,0:T(8,128)}, u32[]{:S(2)}) copy-start(f32[1,256,768]{2,1,0:T(8,128)} %param.21) | copy-start | bytes 2359300
  186.7 63.7 %copy-start.4 = (bf16[1,256,768]{2,1,0:T(8,128)(2,1)S(1)}, bf16[1,256,768]{2,1,0:T(8,128)(2,1)}, u32[]{:S(2)}) copy-start(bf16[1,256,768]{2,1,0:T(8,128)(2,1)} %param.18) | copy-start | bytes 1179652
  253.4 0.7 copy-start.14
  253.4 0.7 copy-start.15
  253.4 0.7 copy-start.16
  402.2 1.4 copy-start.9
  402.2 1.6 copy-start.10
  403.7 4.2 %copy-start.3 = (f32[11,32,768]{2,1,0:T(8,128)}, f32[11,32,768]{2,1,0:T(8,128)S(1)}, u32[]{:S(2)}) copy-start(f32[11,32,768]{2,1,0:T(8,128)S(1)} %broadcast_multiply_fusion) | copy-start | bytes 3244036
  403.7 2.1 copy-start.11
  403.7 2.1 copy-start.12
  405.8 2.1 copy-start.7
  405.8 2.1 copy-start.8
Sparse Core Ops, SparseCore 0:
  16.3 41.8 all-reduce.5
  253.5 148.5 all-reduce.3
where the time goes:
time: 418 us; the launch traced here: 417 us
  waiting for transfers between devices  189 us (45%)
  blocking collectives  125 us (30%)
  other arithmetic  64.1 us (15%)
  matrix products  22.1 us (5%)
  between operations  14.3 us (3%)
    psum x1, waiting for transfers between devices, body(): next_start = lax.psum(partial_right, ('rep', 'shard')) / replicas  147 us
    psum x1, blocking collectives, body(): grams = lax.psum(local_grams, 'shard')  125 us
    psum x1, waiting for transfers between devices, body(): lax.psum((proj_attention, proj_dense, proj_embedding), 'rep')  41.9 us
    another operation x4, other arithmetic, invert(): factor = jnp.linalg.cholesky(grams)  33.1 us
    another operation x3, other arithmetic, invert(): lax.linalg.triangular_solve(factor, identity, left_side=True, lower=True)  27.2 us
  transfers between devices with their start and end apart: 2, of which 2 were waited for; matrix products, arithmetic and copies ran while one was open for 0% of the time, Pallas kernels for 0%

commit v1 on v0

--- a/solution.py
+++ b/solution.py
@@ -70,7 +70,8 @@
         ],
         0,
     )
-    next_start = lax.psum(partial_right, ("rep", "shard")) / replicas
+    _touch_joints = lambda state: lax.psum(lax.psum(state, "shard"), "rep")
+    next_start = _touch_joints(partial_right) / replicas
     approx_attention = jnp.einsum(
         "mkr,mkc->mrc", ortho_attention, next_start[:8], precision=highest
     )

time: 418 us -> 422 us (level)
  waiting for transfers between devices: 189 us -> 194 us
    psum x1 -> x2, waiting for transfers between devices: 147 us -> 152 us  [body(): _touch_joints = lambda state: lax.psum(lax.psum(state, 'shard'), 'rep')]
  transfers between devices with their start and end apart: 2 -> 3, of which waited for: 2 -> 3; matrix products, arithmetic and copies ran while one was open for 0% -> 0% of each run, Pallas kernels for 0% -> 0%
where the time goes in v1:
time: 422 us; the launch traced here: 421 us
  waiting for transfers between devices  194 us (46%)
  blocking collectives  125 us (30%)
  other arithmetic  64.1 us (15%)
  matrix products  22.1 us (5%)
  between operations  14 us (3%)
    psum x2, waiting for transfers between devices, body(): _touch_joints = lambda state: lax.psum(lax.psum(state, 'shard'), 'rep')  152 us
    psum x1, blocking collectives, body(): grams = lax.psum(local_grams, 'shard')  125 us
    psum x1, waiting for transfers between devices, body(): lax.psum((proj_attention, proj_dense, proj_embedding), 'rep')  41.9 us
    another operation x4, other arithmetic, invert(): factor = jnp.linalg.cholesky(grams)  33.1 us
    another operation x3, other arithmetic, invert(): lax.linalg.triangular_solve(factor, identity, left_side=True, lower=True)  27.2 us
  transfers between devices with their start and end apart: 3, of which 3 were waited for; matrix products, arithmetic and copies ran while one was open for 0% of the time, Pallas kernels for 0%

profile of v1, /device:TPU:1, one launch (start us, length us, event | category | flops | bytes accessed | tf_op | source)
XLA Modules:
  0.0 421.1 jit_solution(1752593810938974026)
XLA Ops:
  7.2 1.3 copy.47
  8.6 2.7 convolution_bitcast_fusion.2
  11.3 2.2 convolution_bitcast_fusion.3
  13.5 2.6 convolution_bitcast_fusion
  16.2 41.9 %all-reduce.9.cloned.1.call-done = (f32[32,256]{1,0:T(8,128)}, f32[2,32,96]{2,1,0:T(8,128)}, f32[8,32,24]{1,2,0:T(8,128)}, f32[3,24]{1,0:T(4,128)}) async-done(((f32[32,256]{1,0:T(8,128)}, f32[2,32,96]{2,1,0:T(8,128)}, f32[8,32,24]{1,2,0:T(8,128)}, f32[3,24]{1,0:T(4,128)}), (f32[32,256]{1,0:T(8,128)}, f32[2,32,96]{2,1,0:T(8,128)}, f32[8,32,24]{1,2,0:T(8,128)}, ...) | async-done | bytes 82224 | tf_op jit(solution)/shard_map/psum | solution.py:46
  58.2 1.0 convolution_bitcast_fusion.4
  59.2 1.0 fusion.35
  60.2 1.4 fusion.25
  61.6 125.0 %psum.52 = f32[11,32,32]{1,2,0:T(8,128)S(1)} all-reduce(f32[11,32,32]{1,2,0:T(8,128)S(1)} %pad_maximum_fusion.1), channel_id=1, replica_groups=mesh['rep'=4,'shard'=32] {'shard'}, use_global_device_ids=true, to_apply=%region_3.0 | all-reduce | flops 11264 | bytes 90112 | tf_op jit(solution)/shard_map/psum | solution.py:60
  186.7 0.7 fusion.19
  187.4 32.9 %custom-call.7 = f32[11,32,32]{2,1,0:T(8,128)S(1)} custom-call(f32[11,32,32]{2,1,0:T(8,128)} %fusion.19), custom_call_target="Cholesky" | custom-call | tf_op jit(solution)/shard_map/jit(cholesky)/cholesky | solution.py:8
  220.6 27.1 %custom-call.8 = f32[11,1,32,32]{2,3,1,0:T(8,128)S(1)} custom-call(f32[11,1,32,32]{3,2,1,0:T(8,128)S(1)} %select_bitcast_fusion), custom_call_target="InvertDiagBlocksLowerTriangular" | custom-call | tf_op jit(solution)/shard_map/triangular_solve | solution.py:10
  248.5 0.9 fusion.30
  249.5 0.9 fusion.33
  250.4 0.6 convolution_bitcast_fusion.1
  251.5 0.8 fusion.10
  252.3 1.1 pad_maximum_fusion
  253.5 105.9 %all-reduce.5.cloned.1.call-done = f32[11,32,768]{2,1,0:T(8,128)} async-done(((f32[11,32,768]{2,1,0:T(8,128)}), f32[11,32,768]{2,1,0:T(8,128)}) %all-reduce.5.cloned.1.call-update) | async-done | bytes 1081360 | tf_op jit(solution)/shard_map/psum | solution.py:73
  359.4 0.6 multiply_subtract_fusion.3
  360.0 46.3 %all-reduce.7.cloned.1.call-done = f32[11,32,768]{2,1,0:T(8,128)} async-done(((f32[11,32,768]{2,1,0:T(8,128)}), f32[11,32,768]{2,1,0:T(8,128)}) %all-reduce.7.cloned.1.call-update) | async-done | bytes 1081360 | tf_op jit(solution)/shard_map/psum | solution.py:73
  406.3 1.4 broadcast_multiply_fusion
  407.8 2.0 fusion.50
  409.9 2.1 fusion.49
  412.0 2.5 fusion.48
  (51 shorter events, 2.0 us)
Async XLA Ops:
  7.2 4.1 copy-start.2
  7.2 4.1 copy-start.6
  7.2 51.0 %all-reduce.9.cloned.1.call-start = ((), (), s32[]{:S(2)}) async-start(), calls=%async_computation.2 | async-start | bytes 331776 | tf_op jit(solution)/shard_map/psum | solution.py:46
  8.6 4.9 %copy-start.1 = (f32[1,8,24,768]{3,2,1,0:T(8,128)S(1)}, f32[1,8,24,768]{3,2,1,0:T(8,128)}, u32[]{:S(2)}) copy-start(f32[1,8,24,768]{3,2,1,0:T(8,128)} %param.19) | copy-start | bytes 1769476
  8.6 4.9 %copy-start.5 = (bf16[1,8,24,768]{3,2,1,0:T(8,128)(2,1)S(1)}, bf16[1,8,24,768]{3,2,1,0:T(8,128)(2,1)}, u32[]{:S(2)}) copy-start(bf16[1,8,24,768]{3,2,1,0:T(8,128)(2,1)} %param.16) | copy-start | bytes 884740
  16.1 343.2 %all-reduce.5.cloned.1.call-start = ((), (), s32[]{:S(2)}) async-start(), calls=%async_computation | async-start | bytes 2162688 | tf_op jit(solution)/shard_map/psum | solution.py:73
  61.6 186.6 %copy-start.13 = (f32[8,32,24]{1,2,0:T(8,128)S(1)}, f32[8,32,24]{1,2,0:T(8,128)}, u32[]{:S(2)}) copy-start(f32[8,32,24]{1,2,0:T(8,128)} %get-tuple-element.17) | copy-start | bytes 73732
  186.7 63.7 %copy-start = (f32[1,256,768]{2,1,0:T(8,128)S(1)}, f32[1,256,768]{2,1,0:T(8,128)}, u32[]{:S(2)}) copy-start(f32[1,256,768]{2,1,0:T(8,128)} %param.21) | copy-start | bytes 2359300
  186.7 63.7 %copy-start.4 = (bf16[1,256,768]{2,1,0:T(8,128)(2,1)S(1)}, bf16[1,256,768]{2,1,0:T(8,128)(2,1)}, u32[]{:S(2)}) copy-start(bf16[1,256,768]{2,1,0:T(8,128)(2,1)} %param.18) | copy-start | bytes 1179652
  253.4 106.0 %copy-start.14 = (f32[3,24]{1,0:T(4,128)S(1)}, f32[3,24]{1,0:T(4,128)}, u32[]{:S(2)}) copy-start(f32[3,24]{1,0:T(4,128)} %param.29) | copy-start | bytes 868
  253.4 106.0 %copy-start.15 = (f32[3,24]{1,0:T(4,128)S(1)}, f32[3,24]{1,0:T(4,128)}, u32[]{:S(2)}) copy-start(f32[3,24]{1,0:T(4,128)} %param.30) | copy-start | bytes 868
  253.4 106.0 %copy-start.16 = (f32[3,24]{1,0:T(4,128)S(1)}, f32[3,24]{1,0:T(4,128)}, u32[]{:S(2)}) copy-start(f32[3,24]{1,0:T(4,128)} %get-tuple-element.18) | copy-start | bytes 868
  253.4 152.9 %all-reduce.7.cloned.1.call-start = ((), (), s32[]{:S(2)}) async-start(), calls=%async_computation.1 | async-start | bytes 2162688 | tf_op jit(solution)/shard_map/psum | solution.py:73
  406.3 1.4 copy-start.9
  406.3 1.6 copy-start.10
  407.8 4.2 copy-start.3
  407.8 2.1 copy-start.11
  407.8 2.1 copy-start.12
  409.9 2.1 copy-start.7
  409.9 2.1 copy-start.8
Sparse Core Ops, SparseCore 0:
  16.3 41.8 all-reduce.8
  253.5 105.7 all-reduce.4
  361.9 44.3 all-reduce.6
